TPU v7x, 32 devices: a whole 2x2x4 slice. The times are simulated.
32 devices in a mesh: clips: 2 (over y), space: 4 (over z), tm: 2 (over x), chan: 2 (over core).
Axes of the slice: x: 2, y: 2, z: 4, core: 2. Of those that a mesh axis runs over, the one named last changes fastest.
Arguments:
- frames_in: bfloat16 [4, 16, 160, 384], P(('clips', 'tm'), 'space', None, 'chan'), parts along dimension 0, may hold values from -6 to 6
- cache: bfloat16 [4, 16, 160, 384], P('clips', 'space'), parts along dimension 0, may hold values from -6 to 6
- gain_one: bfloat16 [384], replicated, may hold values from 0.099609375 to 1.8984375
- gain_two: bfloat16 [384], replicated, may hold values from 0.099609375 to 1.8984375
- w_query: bfloat16 [384, 384], replicated, may hold values from -10 to 10
- w_key: bfloat16 [384, 384], replicated, may hold values from -10 to 10
- w_value: bfloat16 [384, 384], replicated, may hold values from -0.3125 to 0.3125
- w_out: bfloat16 [384, 384], replicated, may hold values from -0.3125 to 0.3125
- conv_weight: bfloat16 [3, 3, 3, 384, 384], P(None, None, None, None, 'chan'), may hold values from -0.0625 to 0.0625
Outputs:
- decoded: bfloat16 [4, 16, 160, 384], P(('clips', 'tm'), 'space', None, 'chan'), parts along dimension 0
There are 2 independent parts, one for each index of `clips`. A program takes and returns all parts, laid end to end along the dimension named above; an argument that names none is the same for every part. Nothing has to cross between parts.
All inputs are finite; a program needn't handle non-finite values.
Results may differ from a plain program's by a relative error of at most 0.0062.
Values may be sent and summed in bfloat16 or wider, within the bound.
A program may use at most 128 MiB of HBM per device.

v0:
```python
import jax
import jax.numpy as jnp
from jax import lax
from jax.sharding import PartitionSpec as P


def from_behind(array, axis, by):
    devices = lax.axis_size(axis)
    pairs = [(i, i + by) for i in range(devices) if 0 <= i + by < devices]
    return lax.ppermute(array, axis, pairs)


def padded_2(cells, sides, width):
    for axis, dim in sides:
        count = lax.axis_size(axis)
        ends = count - 1
        head = lax.slice_in_dim(cells, 0, width, axis=dim)
        tail = lax.slice_in_dim(cells, cells.shape[dim] - width, cells.shape[dim], axis=dim)
        cells = jnp.concatenate(
            [
                lax.ppermute(tail, axis, [(i, (i + 1) % count) for i in range(ends)]),
                cells,
                lax.ppermute(head, axis, [((i + 1) % count, i) for i in range(ends)]),
            ],
            axis=dim,
        )
    return cells


def rms_scaled(values, gain):
    wide = values.astype(jnp.float32)
    factor = lax.rsqrt(jnp.mean(wide * wide, axis=-1, keepdims=True) + 1e-06)
    return wide * factor * gain.astype(jnp.float32)


def body(frames_in, cache, gain_one, gain_two, w_query, w_key, w_value, w_out, conv_weight):
    mine = lax.axis_index("chan")
    own = lax.all_to_all(frames_in, "chan", split_axis=1, concat_axis=3, tiled=True)
    half_rows, cells, width = (own.shape[1], own.shape[2], own.shape[3])
    tokens = own.reshape(half_rows * cells, width)
    normed = rms_scaled(tokens, gain_one).astype(jnp.bfloat16)
    query = jnp.dot(normed, w_query, preferred_element_type=jnp.float32).astype(jnp.bfloat16)
    scale = width ** (-0.5)
    count = tokens.shape[0]
    piece = lax.all_gather(normed, ("space", "chan"), axis=0, tiled=True)
    keys = jnp.dot(piece, w_key, preferred_element_type=jnp.float32).astype(jnp.bfloat16)
    values = jnp.dot(piece, w_value, preferred_element_type=jnp.float32).astype(jnp.bfloat16)
    top = jnp.full((count, 1), -1e30, jnp.float32)
    scores = jnp.einsum("qc,kc->qk", query, keys, preferred_element_type=jnp.float32) * scale
    new_top = jnp.maximum(top, jnp.max(scores, axis=-1, keepdims=True))
    weights = jnp.exp(scores - new_top)
    total = jnp.sum(weights, axis=-1, keepdims=True)
    accum = jnp.dot(weights.astype(jnp.bfloat16), values, preferred_element_type=jnp.float32)
    top, total, accum = (new_top, total, accum)
    attended = (accum / total).astype(jnp.bfloat16)
    joined = tokens.astype(jnp.float32) + jnp.dot(
        attended, w_out, preferred_element_type=jnp.float32
    )
    joined = joined.astype(jnp.bfloat16).reshape(1, half_rows, cells, width)
    whole = lax.all_gather(joined, "chan", axis=1, tiled=True)
    act = jax.nn.silu(rms_scaled(whole, gain_two)).astype(jnp.bfloat16)
    moment = lax.axis_index("tm")
    first = from_behind(act, "tm", 1)
    second = from_behind(act, "tm", 2)
    prev_one = jnp.where(moment == 0, cache[1:2], first)
    prev_two = jnp.where(moment == 0, cache[0:1], jnp.where(moment == 1, cache[1:2], second))
    stacked = jnp.concatenate([prev_two, prev_one, act], axis=0)
    rimmed = padded_2(stacked, (("space", 1),), 1)
    padded = jnp.pad(rimmed, ((0, 0), (0, 0), (1, 1), (0, 0)))
    conv = lax.conv_general_dilated(
        padded[None],
        conv_weight,
        (1, 1, 1),
        "VALID",
        dimension_numbers=("NDHWC", "DHWIO", "NDHWC"),
        preferred_element_type=jnp.float32,
    )[0]
    share = conv_weight.shape[4]
    own_joined = lax.dynamic_slice_in_dim(whole, mine * share, share, 3)
    return (own_joined.astype(jnp.float32) + conv).astype(jnp.bfloat16)


def solution(mesh):
    return jax.shard_map(
        body,
        mesh=mesh,
        in_specs=(
            P(("clips", "tm"), "space", None, "chan"),
            P("clips", "space", None, None),
            P(),
            P(),
            P(),
            P(),
            P(),
            P(),
            P(None, None, None, None, "chan"),
        ),
        out_specs=P(("clips", "tm"), "space", None, "chan"),
        check_vma=False,
    )
```

profile of v0, /device:TPU:0, one launch (start us, length us, event | category | flops | bytes accessed | tf_op | source)
XLA Modules:
  0.0 116.3 jit_solution(1926624197613109839)
XLA Ops:
  6.5 0.0 copy-start
  6.5 0.0 copy-start.4
  6.5 0.0 copy-start.5
  6.5 0.0 copy-start.2
  6.5 0.0 all-gather.2.cloned.1.call-start
  6.6 5.2 %all_to_all.4 = bf16[1,4,160,192]{3,2,0,1:T(8,128)(2,1)S(1)} all-to-all(bf16[1,4,160,192]{3,2,0,1:T(8,128)(2,1)} %bitcast.55), channel_id=1, replica_groups=mesh['clips'=2,'space'=4,'tm'=2,'chan'=2] {'chan'}, dimensions={1} | all-to-all | bytes 491520 | tf_op jit(solution)/shard_map/all_to_all | solution.py:38
  11.8 0.3 copy.58
  12.1 0.5 reshape.60
  12.6 0.2 multiply_reduce_fusion
  12.9 0.1 rsqrt.20
  13.0 0.0 copy-done.4
  13.0 0.8 multiply_convert_fusion
  13.8 0.0 all-gather.2.cloned.1.call-update
  13.8 0.0 copy-done.5
  13.8 0.0 copy-done.2
  13.8 1.3 %convolution_convert_fusion.2 = bf16[320,384]{1,0:T(8,128)(2,1)S(1)} fusion(bf16[320,384]{1,0:T(8,128)(2,1)} %multiply_convert_fusion, bf16[384,384]{1,0:T(8,128)(2,1)S(1)} %copy-done.2), kind=kOutput, calls=%fused_computation.32 | convolution fusion | flops 94494720 | bytes 786432 | tf_op jit(solution)/shard_map/dot_general | solution.py:42
  15.1 29.6 %all-gather.2.cloned.1.call-done = bf16[2560,384]{1,0:T(8,128)(2,1)} async-done(((bf16[320,384]{1,0:T(8,128)(2,1)}), bf16[2560,384]{1,0:T(8,128)(2,1)}) %all-gather.2.cloned.1.call-update) | async-done | bytes 1966096 | tf_op jit(solution)/shard_map/all_gather | solution.py:45
  44.7 0.0 copy-done
  44.7 5.4 %fusion.46 = (f32[320]{0:T(512)S(1)}, f32[320,2560]{1,0:T(8,128)}) fusion(bf16[320,384]{1,0:T(8,128)(2,1)S(1)} %convolution_convert_fusion.2, bf16[2560,384]{1,0:T(8,128)(2,1)} %all-gather.2.cloned.1.call-done, bf16[384,384]{1,0:T(8,128)(2,1)S(1)} %copy-done), kind=kOutput, calls=%fused_computation.64 | convolution fusion | flops 1386741504 | bytes 5784832 | tf_op jit(solution)/shard_map/qc,kc->qk/dot_general | solution.py:49
  50.1 0.0 copy-start.7
  50.1 2.6 %fusion.2 = f32[320]{0:T(512)S(1)} fusion(f32[320,2560]{1,0:T(8,128)} %get-tuple-element.10, f32[320]{0:T(512)S(1)} %broadcast_maximum_fusion), kind=kLoop, calls=%fused_computation.9 | loop fusion | flops 1638080 | bytes 3279360 | tf_op jit(solution)/shard_map/reduce_sum | solution.py:52
  52.7 0.0 copy-done.7
  52.7 0.0 copy-start.3
  52.7 4.8 %fusion.28 = bf16[320,384]{1,0:T(8,128)(2,1)S(1)} fusion(f32[320,2560]{1,0:T(8,128)} %get-tuple-element.10, f32[320]{0:T(512)S(1)} %broadcast_maximum_fusion, bf16[2560,384]{1,0:T(8,128)(2,1)} %all-gather.2.cloned.1.call-done, bf16[384,384]{1,0:T(8,128)(2,1)S(1)} %copy-done.7, f32[320]{0:T(512)S(1)} %fusion.2), kind=kOutput, calls=%fused_computation.35 | convolution fusion | flops 1386987520 | bytes 5786112 | tf_op jit(solution)/shard_map/dot_general | solution.py:53
  57.5 0.0 copy-done.3
  57.5 0.0 copy-start.1
  57.5 0.3 fusion.24
  57.9 2.2 %all_gather.7 = bf16[1,4,160,384]{3,2,0,1:T(8,128)(2,1)S(1)} all-gather(bf16[1,2,160,384]{3,2,0,1:T(8,128)(2,1)S(1)} %bitcast.53), channel_id=1, replica_groups=mesh['clips'=2,'space'=4,'tm'=2,'chan'=2] {'chan'}, dimensions={1}, use_global_device_ids=true | all-gather | bytes 737280 | tf_op jit(solution)/shard_map/all_gather | solution.py:60
  60.0 0.2 fusion.31
  60.3 0.4 fusion.38
  60.6 1.4 %collective-permute-start = (bf16[1,4,160,384]{3,2,0,1:T(8,128)(2,1)S(1)}, bf16[1,4,160,384]{3,2,0,1:T(8,128)(2,1)}, u32[]{:S(2)}, u32[]{:S(2)}) collective-permute-start(bf16[1,4,160,384]{3,2,0,1:T(8,128)(2,1)S(1)} %fusion.38), channel_id=1, source_target_pairs={} | collective-permute-start | bytes 1474568 | tf_op jit(solution)/shard_map/ppermute | solution.py:10
  62.1 4.2 %collective-permute-start.1 = (bf16[1,4,160,384]{3,2,0,1:T(8,128)(2,1)S(1)}, bf16[1,4,160,384]{3,2,0,1:T(8,128)(2,1)}, u32[]{:S(2)}, u32[]{:S(2)}) collective-permute-start(bf16[1,4,160,384]{3,2,0,1:T(8,128)(2,1)S(1)} %fusion.38), channel_id=1, source_target_pairs={{0,2},{1,3},{4,6},{5,7},{8,10},{9,11},{12,14},{13,15},{16,18},{17,... | collective-permute-start | bytes 1474568 | tf_op jit(solution)/shard_map/ppermute | solution.py:10
  66.2 0.0 collective-permute-done
  66.2 10.1 %collective-permute-done.1 = bf16[1,4,160,384]{3,2,0,1:T(8,128)(2,1)} collective-permute-done((bf16[1,4,160,384]{3,2,0,1:T(8,128)(2,1)S(1)}, bf16[1,4,160,384]{3,2,0,1:T(8,128)(2,1)}, u32[]{:S(2)}, u32[]{:S(2)}) %collective-permute-start.1) | collective-permute-done | bytes 491552 | tf_op jit(solution)/shard_map/ppermute | solution.py:10
  76.3 0.0 copy-done.1
  76.3 1.1 fusion.41
  77.5 1.0 maximum_bitcast_fusion
  78.4 3.5 %collective-permute-start.2 = (bf16[3,1,160,384]{3,2,1,0:T(8,128)(2,1)}, bf16[3,1,160,384]{3,2,1,0:T(8,128)(2,1)S(1)}, u32[]{:S(2)}, u32[]{:S(2)}) collective-permute-start(bf16[3,1,160,384]{3,2,1,0:T(8,128)(2,1)} %get-tuple-element.5), channel_id=1, source_target_pairs={{0,4},{4,8},{8,12},{1,5},{5,9},{9,13},{2,6},{6,10},{10,14},{3,7},{... | collective-permute-start | bytes 1105928 | tf_op jit(solution)/shard_map/ppermute | solution.py:21
  81.9 1.5 %collective-permute-start.3 = (bf16[3,1,160,384]{3,2,1,0:T(8,128)(2,1)}, bf16[3,1,160,384]{3,2,1,0:T(8,128)(2,1)}, u32[]{:S(2)}, u32[]{:S(2)}) collective-permute-start(bf16[3,1,160,384]{3,2,1,0:T(8,128)(2,1)} %get-tuple-element.6), channel_id=1, source_target_pairs={{4,0},{8,4},{12,8},{5,1},{9,5},{13,9},{6,2},{10,6},{14,10},{7,3},{... | collective-permute-start | bytes 1105928 | tf_op jit(solution)/shard_map/ppermute | solution.py:23
  83.4 0.2 constant_dynamic-slice_fusion
  83.6 6.1 %collective-permute-done.2 = bf16[3,1,160,384]{3,2,1,0:T(8,128)(2,1)S(1)} collective-permute-done((bf16[3,1,160,384]{3,2,1,0:T(8,128)(2,1)}, bf16[3,1,160,384]{3,2,1,0:T(8,128)(2,1)S(1)}, u32[]{:S(2)}, u32[]{:S(2)}) %collective-permute-start.2) | collective-permute-done | bytes 368672 | tf_op jit(solution)/shard_map/ppermute | solution.py:21
  89.7 4.1 %collective-permute-done.3 = bf16[3,1,160,384]{3,2,1,0:T(8,128)(2,1)} collective-permute-done((bf16[3,1,160,384]{3,2,1,0:T(8,128)(2,1)}, bf16[3,1,160,384]{3,2,1,0:T(8,128)(2,1)}, u32[]{:S(2)}, u32[]{:S(2)}) %collective-permute-start.3) | collective-permute-done | bytes 368672 | tf_op jit(solution)/shard_map/ppermute | solution.py:23
  93.8 3.1 %fusion.11 = bf16[3,6,1,162,384]{4,3,0,1,2:T(8,128)(2,1)S(1)} fusion(bf16[3,1,160,384]{3,2,0,1:T(8,128)(2,1)} %bitcast.8, bf16[3,1,160,384]{3,2,0,1:T(8,128)(2,1)S(1)} %bitcast.54, bf16[1,4,160,384]{3,2,0,1:T(8,128)(2,1)S(1)} %fusion.38, bf16[1,4,160,384]{3,2,0,1:T(8,128)(2,1)S(1)} %get-tuple-element.8, bf16[1,4,160,384]{3,2,0,1:T(8,128)(2,1)S(1)} %get-tuple-element.7), kind=kLoop, calls=%fused_computation.18 | loop fusion | flops 20155392 | bytes 4451328 | tf_op jit(solution)/shard_map/broadcast_in_dim | solution.py:71
  96.9 1.6 %pad.5 = bf16[3,6,1,168,384]{4,3,0,1,2:T(8,128)(2,1)} pad(bf16[3,6,1,162,384]{4,3,0,1,2:T(8,128)(2,1)S(1)} %fusion.11, bf16[]{:T(256)} %constant.34.clone.1), padding=0_0x0_0x0_0x0_6x0_0 | pad | bytes 4561922 | tf_op jit(solution)/shard_map/broadcast_in_dim | solution.py:71
  98.5 3.5 %reshape.69 = bf16[3,6,1,8,21,384]{5,4,3,0,1,2:T(8,128)(2,1)S(1)} reshape(bf16[3,6,1,168,384]{4,3,0,1,2:T(8,128)(2,1)} %pad.5) | data formatting | bytes 4644864 | tf_op jit(solution)/shard_map/conv_general_dilated | solution.py:70
  102.0 0.0 copy-start.6
  102.0 0.0 copy-start.8
  102.1 0.3 copy.47
  102.4 0.1 slice.19
  102.4 1.7 %copy-done.6 = bf16[3,3,3,384,192]{3,4,2,1,0:T(8,128)(2,1)S(1)} copy-done((bf16[3,3,3,384,192]{3,4,2,1,0:T(8,128)(2,1)S(1)}, bf16[3,3,3,384,192]{3,4,2,1,0:T(8,128)(2,1)}, u32[]{:S(2)}) %copy-start.6) | copy-done | bytes 3981336
  104.2 0.0 copy-done.8
  104.2 3.9 %fusion.21 = f32[1,4,8,21,192]{4,2,3,1,0:T(8,128)S(1)} fusion(bf16[3,3,3,384,192]{3,4,2,1,0:T(8,128)(2,1)S(1)} %copy-done.6, bf16[3,6,1,7,2,384]{5,3,4,1,0,2:T(8,128)(2,1)S(1)} %slice.19, bf16[3,6,1,8,21,384]{5,3,4,1,0,2:T(8,128)(2,1)S(1)} %copy.47, pred[8,21]{0,1:T(8,128)(4,1)S(1)} %copy-done.8), kind=kOutput, calls=%fused_computation.28 | convolution fusion | flops 2683201536 | bytes 7013544 | tf_op jit(solution)/shard_map/conv_general_dilated | solution.py:70
  108.1 0.3 copy.48
  108.4 0.3 fusion.40
  108.7 0.8 copy.49
  (7 shorter events, 0.1 us)
Async XLA Ops:
  6.5 38.2 %copy-start = (bf16[384,384]{1,0:T(8,128)(2,1)S(1)}, bf16[384,384]{1,0:T(8,128)(2,1)}, u32[]{:S(2)}) copy-start(bf16[384,384]{1,0:T(8,128)(2,1)} %param.14) | copy-start | bytes 884740
  6.5 6.4 %copy-start.4 = (bf16[384]{0:T(512)(128)(2,1)S(1)}, bf16[384]{0:T(512)(128)(2,1)}, u32[]{:S(2)}) copy-start(bf16[384]{0:T(512)(128)(2,1)} %param.11) | copy-start | bytes 2308
  6.5 7.3 %copy-start.5 = (bf16[384]{0:T(512)(128)(2,1)S(1)}, bf16[384]{0:T(512)(128)(2,1)}, u32[]{:S(2)}) copy-start(bf16[384]{0:T(512)(128)(2,1)} %param.12) | copy-start | bytes 2308
  6.5 7.3 %copy-start.2 = (bf16[384,384]{1,0:T(8,128)(2,1)S(1)}, bf16[384,384]{1,0:T(8,128)(2,1)}, u32[]{:S(2)}) copy-start(bf16[384,384]{1,0:T(8,128)(2,1)} %param.13) | copy-start | bytes 884740
  6.5 38.1 %all-gather.2.cloned.1.call-start = ((), (), s32[]{:S(2)}) async-start(), calls=%async_computation.1 | async-start | bytes 2211840 | tf_op jit(solution)/shard_map/all_gather | solution.py:45
  50.1 2.6 %copy-start.7 = (bf16[384,384]{1,0:T(8,128)(2,1)S(1)}, bf16[384,384]{1,0:T(8,128)(2,1)}, u32[]{:S(2)}) copy-start(bf16[384,384]{1,0:T(8,128)(2,1)} %param.15) | copy-start | bytes 884740
  52.7 4.8 %copy-start.3 = (bf16[384,384]{1,0:T(8,128)(2,1)S(1)}, bf16[384,384]{1,0:T(8,128)(2,1)}, u32[]{:S(2)}) copy-start(bf16[384,384]{1,0:T(8,128)(2,1)} %param.16) | copy-start | bytes 884740
  57.5 18.8 %copy-start.1 = (bf16[2,4,160,384]{3,2,1,0:T(8,128)(2,1)S(1)}, bf16[2,4,160,384]{3,2,1,0:T(8,128)(2,1)}, u32[]{:S(2)}) copy-start(bf16[2,4,160,384]{3,2,1,0:T(8,128)(2,1)} %param.10) | copy-start | bytes 2949124
  60.6 5.6 %collective-permute-start = (bf16[1,4,160,384]{3,2,0,1:T(8,128)(2,1)S(1)}, bf16[1,4,160,384]{3,2,0,1:T(8,128)(2,1)}, u32[]{:S(2)}, u32[]{:S(2)}) collective-permute-start(bf16[1,4,160,384]{3,2,0,1:T(8,128)(2,1)S(1)} %fusion.38), channel_id=1, source_target_pairs={} | collective-permute-start | bytes 1474568 | tf_op jit(solution)/shard_map/ppermute | solution.py:10
  62.1 14.2 %collective-permute-start.1 = (bf16[1,4,160,384]{3,2,0,1:T(8,128)(2,1)S(1)}, bf16[1,4,160,384]{3,2,0,1:T(8,128)(2,1)}, u32[]{:S(2)}, u32[]{:S(2)}) collective-permute-start(bf16[1,4,160,384]{3,2,0,1:T(8,128)(2,1)S(1)} %fusion.38), channel_id=1, source_target_pairs={{0,2},{1,3},{4,6},{5,7},{8,10},{9,11},{12,14},{13,15},{16,18},{17,... | collective-permute-start | bytes 1474568 | tf_op jit(solution)/shard_map/ppermute | solution.py:10
  78.4 11.2 %collective-permute-start.2 = (bf16[3,1,160,384]{3,2,1,0:T(8,128)(2,1)}, bf16[3,1,160,384]{3,2,1,0:T(8,128)(2,1)S(1)}, u32[]{:S(2)}, u32[]{:S(2)}) collective-permute-start(bf16[3,1,160,384]{3,2,1,0:T(8,128)(2,1)} %get-tuple-element.5), channel_id=1, source_target_pairs={{0,4},{4,8},{8,12},{1,5},{5,9},{9,13},{2,6},{6,10},{10,14},{3,7},{... | collective-permute-start | bytes 1105928 | tf_op jit(solution)/shard_map/ppermute | solution.py:21
  81.9 11.9 %collective-permute-start.3 = (bf16[3,1,160,384]{3,2,1,0:T(8,128)(2,1)}, bf16[3,1,160,384]{3,2,1,0:T(8,128)(2,1)}, u32[]{:S(2)}, u32[]{:S(2)}) collective-permute-start(bf16[3,1,160,384]{3,2,1,0:T(8,128)(2,1)} %get-tuple-element.6), channel_id=1, source_target_pairs={{4,0},{8,4},{12,8},{5,1},{9,5},{13,9},{6,2},{10,6},{14,10},{7,3},{... | collective-permute-start | bytes 1105928 | tf_op jit(solution)/shard_map/ppermute | solution.py:23
  102.0 2.1 %copy-start.6 = (bf16[3,3,3,384,192]{3,4,2,1,0:T(8,128)(2,1)S(1)}, bf16[3,3,3,384,192]{3,4,2,1,0:T(8,128)(2,1)}, u32[]{:S(2)}) copy-start(bf16[3,3,3,384,192]{3,4,2,1,0:T(8,128)(2,1)} %param.17) | copy-start | bytes 11943940
  102.0 2.1 %copy-start.8 = (pred[8,21]{0,1:T(8,128)(4,1)S(1)}, pred[8,21]{0,1:T(8,128)(4,1)}, u32[]{:S(2)}) copy-start(pred[8,21]{0,1:T(8,128)(4,1)} %constant.42) | copy-start | bytes 508
Sparse Core Ops, SparseCore 0:
  13.9 30.7 all-gather.1
where the time goes:
time: 117 us; the launch traced here: 116 us
  waiting for transfers between devices  49.9 us (43%)
  matrix products  15.7 us (13%)
  between operations  13.6 us (12%)
  starting transfers between devices  10.6 us (9%)
  other arithmetic  9.76 us (8%)
  local copies, waits for them, and re-layouts  9.41 us (8%)
  blocking collectives  7.34 us (6%)
    all_gather x1, waiting for transfers between devices, body(): piece = lax.all_gather(normed, ('space', 'chan'), axis=0, tiled=True)  29.6 us
    ppermute x2, waiting for transfers between devices, from_behind(): return lax.ppermute(array, axis, pairs)  10.1 us
    ppermute x1, waiting for transfers between devices, padded_2(): lax.ppermute(tail, axis, [(i, (i + 1) % count) for i in range(ends)])  6.08 us
    ppermute x2, starting transfers between devices, from_behind(): return lax.ppermute(array, axis, pairs)  5.6 us
    dot_general x1, matrix products, body(): jnp.einsum('qc,kc->qk', query, keys, preferred_element_type=jnp.float32)  5.41 us
    all_to_all x1, blocking collectives, body(): lax.all_to_all(frames_in, 'chan', split_axis=1, concat_axis=3, tiled=True)  5.19 us
    dot_general x1, matrix products, body(): jnp.dot(weights.astype(jnp.bfloat16), values, preferred_element_type=jnp....  4.79 us
    ppermute x1, waiting for transfers between devices, padded_2(): lax.ppermute(head, axis, [((i + 1) % count, i) for i in range(ends)])  4.14 us
  transfers between devices with their start and end apart: 5, of which 4 were waited for; matrix products, arithmetic and copies ran while one was open for 1% of the time, Pallas kernels for 0%

commit v1 on v0

--- a/solution.py
+++ b/solution.py
@@ -2,6 +2,25 @@
 import jax.numpy as jnp
 from jax import lax
 from jax.sharding import PartitionSpec as P
+
+
+def joined_along(parts, dim):
+    parts = jnp.moveaxis(parts, 0, dim)
+    shape = parts.shape
+    return parts.reshape(*shape[:dim], shape[dim] * shape[dim + 1], *shape[dim + 2 :])
+
+
+def grow_blocks(x, axis):
+    devices, place = (lax.axis_size(axis), lax.axis_index(axis))
+    parts, stride = (x[None], 1)
+    while stride < devices:
+        partner_block = lax.ppermute(parts, axis, [(i, i ^ stride) for i in range(devices)])
+        low = place & stride == 0
+        parts = jnp.concatenate(
+            [jnp.where(low, parts, partner_block), jnp.where(low, partner_block, parts)]
+        )
+        stride *= 2
+    return parts
 
 
 def from_behind(array, axis, by):
@@ -42,7 +61,7 @@
     query = jnp.dot(normed, w_query, preferred_element_type=jnp.float32).astype(jnp.bfloat16)
     scale = width ** (-0.5)
     count = tokens.shape[0]
-    piece = lax.all_gather(normed, ("space", "chan"), axis=0, tiled=True)
+    piece = joined_along(grow_blocks(normed, ("space", "chan")), 0)
     keys = jnp.dot(piece, w_key, preferred_element_type=jnp.float32).astype(jnp.bfloat16)
     values = jnp.dot(piece, w_value, preferred_element_type=jnp.float32).astype(jnp.bfloat16)
     top = jnp.full((count, 1), -1e30, jnp.float32)

time: 117 us -> 133 us (1.14)
  waiting for transfers between devices: 49.9 us -> 73.7 us
  between operations: 13.6 us -> 0.27 us
  starting transfers between devices: 10.6 us -> 15.5 us
  matrix products: 15.7 us -> 13.7 us
  other arithmetic: 9.76 us -> 11.2 us
    ppermute x0 -> x3, waiting for transfers between devices: none -> 53.6 us  [grow_blocks(): lax.ppermute(parts, axis, [(i, i ^ stride) for i in range(devices)])]
    all_gather x1 -> x0, waiting for transfers between devices: 29.6 us -> none  [body(): piece = lax.all_gather(normed, ('space', 'chan'), axis=0, tiled=True)]
    ppermute x0 -> x3, starting transfers between devices: none -> 6.12 us  [grow_blocks(): lax.ppermute(parts, axis, [(i, i ^ stride) for i in range(devices)])]
    select_n x0 -> x3, other arithmetic: none -> 1.76 us  [grow_blocks(): jnp.where(low, parts, partner_block)]
    dot_general x1, matrix products: 5.41 us -> 3.89 us  [body(): jnp.einsum('qc,kc->qk', query, keys, preferred_element_type=jnp.float32)]
  transfers between devices with their start and end apart: 5 -> 7, of which waited for: 4 -> 6; matrix products, arithmetic and copies ran while one was open for 1% -> 2% of each run, Pallas kernels for 0% -> 0%
where the time goes in v1:
time: 133 us; the launch traced here: 132 us
  waiting for transfers between devices  73.7 us (55%)
  starting transfers between devices  15.5 us (12%)
  matrix products  13.7 us (10%)
  other arithmetic  11.2 us (8%)
  local copies, waits for them, and re-layouts  9.9 us (7%)
  blocking collectives  7.33 us (6%)
    ppermute x3, waiting for transfers between devices, grow_blocks(): lax.ppermute(parts, axis, [(i, i ^ stride) for i in range(devices)])  53.6 us
    ppermute x2, waiting for transfers between devices, from_behind(): return lax.ppermute(array, axis, pairs)  9.99 us
    ppermute x3, starting transfers between devices, grow_blocks(): lax.ppermute(parts, axis, [(i, i ^ stride) for i in range(devices)])  6.12 us
    ppermute x1, waiting for transfers between devices, padded_2(): lax.ppermute(tail, axis, [(i, (i + 1) % count) for i in range(ends)])  5.94 us
    ppermute x2, starting transfers between devices, from_behind(): return lax.ppermute(array, axis, pairs)  5.45 us
    all_to_all x1, blocking collectives, body(): lax.all_to_all(frames_in, 'chan', split_axis=1, concat_axis=3, tiled=True)  5.17 us
    dot_general x1, matrix products, body(): jnp.dot(weights.astype(jnp.bfloat16), values, preferred_element_type=jnp....  4.21 us
    ppermute x1, waiting for transfers between devices, padded_2(): lax.ppermute(head, axis, [((i + 1) % count, i) for i in range(ends)])  4.14 us
  transfers between devices with their start and end apart: 7, of which 6 were waited for; matrix products, arithmetic and copies ran while one was open for 2% of the time, Pallas kernels for 0%

profile of v1, /device:TPU:0, one launch (start us, length us, event | category | flops | bytes accessed | tf_op | source)
XLA Modules:
  0.0 131.6 jit_solution(1793169788023028562)
XLA Ops:
  0.0 0.0 copy-start
  0.0 0.0 copy-start.3
  0.0 5.2 %all_to_all.4 = bf16[1,4,160,192]{3,2,0,1:T(8,128)(2,1)S(1)} all-to-all(bf16[1,4,160,192]{3,2,0,1:T(8,128)(2,1)} %bitcast.58), channel_id=1, replica_groups=mesh['clips'=2,'space'=4,'tm'=2,'chan'=2] {'chan'}, dimensions={1} | all-to-all | bytes 491520 | tf_op jit(solution)/shard_map/all_to_all | solution.py:57
  5.2 0.3 copy.58
  5.5 0.5 reshape.127
  6.0 0.2 multiply_reduce_fusion
  6.3 0.1 rsqrt.20
  6.4 0.0 copy-done.3
  6.4 0.1 multiply_convert_fusion
  6.5 0.2 collective-permute-start
  6.7 1.4 %collective-permute-done = bf16[1,320,384]{2,1,0:T(8,128)(2,1)S(1)} collective-permute-done((bf16[1,320,384]{2,1,0:T(8,128)(2,1)S(1)}, bf16[1,320,384]{2,1,0:T(8,128)(2,1)S(1)}, u32[]{:S(2)}, u32[]{:S(2)}) %collective-permute-start) | collective-permute-done | bytes 245792 | tf_op jit(solution)/shard_map/ppermute | solution.py:17
  8.1 0.2 broadcast_select_fusion.5
  8.3 0.1 pad_maximum_fusion.2
  8.3 3.1 %collective-permute-start.1 = (bf16[2,320,384]{2,1,0:T(8,128)(2,1)S(1)}, bf16[2,320,384]{2,1,0:T(8,128)(2,1)S(1)}, u32[]{:S(2)}, u32[]{:S(2)}) collective-permute-start(bf16[2,320,384]{2,1,0:T(8,128)(2,1)S(1)} %pad_maximum_fusion.2), channel_id=1, source_target_pairs={{0,4},{1,5},{4,0},{5,1},{8,12},{9,13},{12,8},{13,9},{2,6},{3,7},{6... | collective-permute-start | bytes 1474568 | tf_op jit(solution)/shard_map/ppermute | solution.py:17
  11.4 0.0 copy-start.4
  11.4 11.5 %collective-permute-done.1 = bf16[2,320,384]{2,1,0:T(8,128)(2,1)S(1)} collective-permute-done((bf16[2,320,384]{2,1,0:T(8,128)(2,1)S(1)}, bf16[2,320,384]{2,1,0:T(8,128)(2,1)S(1)}, u32[]{:S(2)}, u32[]{:S(2)}) %collective-permute-start.1) | collective-permute-done | bytes 491552 | tf_op jit(solution)/shard_map/ppermute | solution.py:17
  23.0 0.1 broadcast_select_fusion.3
  23.1 0.1 pad_maximum_fusion.1
  23.2 2.8 %collective-permute-start.2 = (bf16[4,320,384]{2,1,0:T(8,128)(2,1)S(1)}, bf16[4,320,384]{2,1,0:T(8,128)(2,1)}, u32[]{:S(2)}, u32[]{:S(2)}) collective-permute-start(bf16[4,320,384]{2,1,0:T(8,128)(2,1)S(1)} %pad_maximum_fusion.1), channel_id=1, source_target_pairs={{0,8},{1,9},{4,12},{5,13},{8,0},{9,1},{12,4},{13,5},{2,10},{3,11},... | collective-permute-start | bytes 2949128 | tf_op jit(solution)/shard_map/ppermute | solution.py:17
  26.0 0.5 reshape.126
  26.5 0.0 copy-done.4
  26.6 1.3 %convolution_convert_fusion.2 = bf16[320,384]{1,0:T(8,128)(2,1)S(1)} fusion(bf16[384,384]{1,0:T(8,128)(2,1)} %param.13, f32[320,384]{1,0:T(8,128)S(1)} %reshape.126, f32[384]{0:T(512)S(1)} %convert_element_type.87, f32[320]{0:T(512)S(1)} %rsqrt.20), kind=kOutput, calls=%fused_computation.33 | convolution fusion | flops 94863360 | bytes 1035008 | tf_op jit(solution)/shard_map/dot_general | solution.py:61
  27.9 40.7 %collective-permute-done.2 = bf16[4,320,384]{2,1,0:T(8,128)(2,1)} collective-permute-done((bf16[4,320,384]{2,1,0:T(8,128)(2,1)S(1)}, bf16[4,320,384]{2,1,0:T(8,128)(2,1)}, u32[]{:S(2)}, u32[]{:S(2)}) %collective-permute-start.2) | collective-permute-done | bytes 983072 | tf_op jit(solution)/shard_map/ppermute | solution.py:17
  68.6 1.5 %broadcast_select_fusion.1 = (bf16[4,320,384]{2,1,0:T(8,128)(2,1)S(1)}, bf16[4,320,384]{2,1,0:T(8,128)(2,1)S(1)}) fusion(bf16[4,320,384]{2,1,0:T(8,128)(2,1)} %collective-permute-done.2, pred[]{:T(512)S(6)} %eq.16, bf16[2,320,384]{2,1,0:T(8,128)(2,1)S(1)} %get-tuple-element.12, bf16[2,320,384]{2,1,0:T(8,128)(2,1)S(1)} %get-tuple-element.11), kind=kLoop, calls=%fused_computation.47 | loop fusion | flops 1474560 | bytes 3932161 | tf_op jit(solution)/shard_map/jit(_where)/select_n | solution.py:20
  70.1 0.2 pad_maximum_fusion
  70.3 0.0 copy-done
  70.3 3.9 %fusion.48 = (f32[320]{0:T(512)S(1)}, f32[320,2560]{1,0:T(8,128)}) fusion(bf16[320,384]{1,0:T(8,128)(2,1)S(1)} %convolution_convert_fusion.2, bf16[2560,384]{1,0:T(8,128)(2,1)S(1)} %bitcast.54, bf16[384,384]{1,0:T(8,128)(2,1)S(1)} %copy-done), kind=kOutput, calls=%fused_computation.76 | convolution fusion | flops 1386741504 | bytes 5784832 | tf_op jit(solution)/shard_map/qc,kc->qk/dot_general | solution.py:68
  74.2 2.5 %fusion.2 = f32[320]{0:T(512)S(1)} fusion(f32[320,2560]{1,0:T(8,128)} %get-tuple-element.16, f32[320]{0:T(512)S(1)} %broadcast_maximum_fusion), kind=kLoop, calls=%fused_computation.9 | loop fusion | flops 1638080 | bytes 3279360 | tf_op jit(solution)/shard_map/reduce_sum | solution.py:71
  76.8 0.0 copy-start.2
  76.8 4.2 %fusion.28 = bf16[320,384]{1,0:T(8,128)(2,1)S(1)} fusion(f32[320,2560]{1,0:T(8,128)} %get-tuple-element.16, f32[320]{0:T(512)S(1)} %broadcast_maximum_fusion, bf16[2560,384]{1,0:T(8,128)(2,1)S(1)} %bitcast.55, bf16[384,384]{1,0:T(8,128)(2,1)} %param.15, f32[320]{0:T(512)S(1)} %fusion.2), kind=kOutput, calls=%fused_computation.36 | convolution fusion | flops 1386987520 | bytes 5786112 | tf_op jit(solution)/shard_map/dot_general | solution.py:72
  81.0 0.0 copy-done.2
  81.0 0.0 copy-start.1
  81.0 0.3 fusion.24
  81.3 2.2 %all_gather.3 = bf16[1,4,160,384]{3,2,0,1:T(8,128)(2,1)S(1)} all-gather(bf16[1,2,160,384]{3,2,0,1:T(8,128)(2,1)S(1)} %bitcast.56), channel_id=1, replica_groups=mesh['clips'=2,'space'=4,'tm'=2,'chan'=2] {'chan'}, dimensions={1}, use_global_device_ids=true | all-gather | bytes 737280 | tf_op jit(solution)/shard_map/all_gather | solution.py:79
  83.5 0.2 fusion.31
  83.7 0.4 fusion.38
  84.1 1.4 %collective-permute-start.3 = (bf16[1,4,160,384]{3,2,0,1:T(8,128)(2,1)S(1)}, bf16[1,4,160,384]{3,2,0,1:T(8,128)(2,1)}, u32[]{:S(2)}, u32[]{:S(2)}) collective-permute-start(bf16[1,4,160,384]{3,2,0,1:T(8,128)(2,1)S(1)} %fusion.38), channel_id=1, source_target_pairs={} | collective-permute-start | bytes 1474568 | tf_op jit(solution)/shard_map/ppermute | solution.py:29
  85.6 4.0 %collective-permute-start.4 = (bf16[1,4,160,384]{3,2,0,1:T(8,128)(2,1)S(1)}, bf16[1,4,160,384]{3,2,0,1:T(8,128)(2,1)}, u32[]{:S(2)}, u32[]{:S(2)}) collective-permute-start(bf16[1,4,160,384]{3,2,0,1:T(8,128)(2,1)S(1)} %fusion.38), channel_id=1, source_target_pairs={{0,2},{1,3},{4,6},{5,7},{8,10},{9,11},{12,14},{13,15},{16,18},{17,... | collective-permute-start | bytes 1474568 | tf_op jit(solution)/shard_map/ppermute | solution.py:29
  89.6 0.0 collective-permute-done.3
  89.6 10.0 %collective-permute-done.4 = bf16[1,4,160,384]{3,2,0,1:T(8,128)(2,1)} collective-permute-done((bf16[1,4,160,384]{3,2,0,1:T(8,128)(2,1)S(1)}, bf16[1,4,160,384]{3,2,0,1:T(8,128)(2,1)}, u32[]{:S(2)}, u32[]{:S(2)}) %collective-permute-start.4) | collective-permute-done | bytes 491552 | tf_op jit(solution)/shard_map/ppermute | solution.py:29
  99.6 0.0 copy-done.1
  99.6 1.1 fusion.41
  100.7 1.0 maximum_bitcast_fusion
  101.7 2.5 %collective-permute-start.5 = (bf16[3,1,160,384]{3,2,1,0:T(8,128)(2,1)}, bf16[3,1,160,384]{3,2,1,0:T(8,128)(2,1)S(1)}, u32[]{:S(2)}, u32[]{:S(2)}) collective-permute-start(bf16[3,1,160,384]{3,2,1,0:T(8,128)(2,1)} %get-tuple-element.7), channel_id=1, source_target_pairs={{0,4},{4,8},{8,12},{1,5},{5,9},{9,13},{2,6},{6,10},{10,14},{3,7},{... | collective-permute-start | bytes 1105928 | tf_op jit(solution)/shard_map/ppermute | solution.py:40
  104.2 1.5 %collective-permute-start.6 = (bf16[3,1,160,384]{3,2,1,0:T(8,128)(2,1)}, bf16[3,1,160,384]{3,2,1,0:T(8,128)(2,1)}, u32[]{:S(2)}, u32[]{:S(2)}) collective-permute-start(bf16[3,1,160,384]{3,2,1,0:T(8,128)(2,1)} %get-tuple-element.8), channel_id=1, source_target_pairs={{4,0},{8,4},{12,8},{5,1},{9,5},{13,9},{6,2},{10,6},{14,10},{7,3},{... | collective-permute-start | bytes 1105928 | tf_op jit(solution)/shard_map/ppermute | solution.py:42
  105.7 0.2 constant_dynamic-slice_fusion
  105.8 5.9 %collective-permute-done.5 = bf16[3,1,160,384]{3,2,1,0:T(8,128)(2,1)S(1)} collective-permute-done((bf16[3,1,160,384]{3,2,1,0:T(8,128)(2,1)}, bf16[3,1,160,384]{3,2,1,0:T(8,128)(2,1)S(1)}, u32[]{:S(2)}, u32[]{:S(2)}) %collective-permute-start.5) | collective-permute-done | bytes 368672 | tf_op jit(solution)/shard_map/ppermute | solution.py:40
  111.8 4.1 %collective-permute-done.6 = bf16[3,1,160,384]{3,2,1,0:T(8,128)(2,1)} collective-permute-done((bf16[3,1,160,384]{3,2,1,0:T(8,128)(2,1)}, bf16[3,1,160,384]{3,2,1,0:T(8,128)(2,1)}, u32[]{:S(2)}, u32[]{:S(2)}) %collective-permute-start.6) | collective-permute-done | bytes 368672 | tf_op jit(solution)/shard_map/ppermute | solution.py:42
  115.9 3.1 %fusion.11 = bf16[3,6,1,162,384]{4,3,0,1,2:T(8,128)(2,1)S(1)} fusion(bf16[3,1,160,384]{3,2,0,1:T(8,128)(2,1)} %bitcast.9, bf16[3,1,160,384]{3,2,0,1:T(8,128)(2,1)S(1)} %bitcast.57, bf16[1,4,160,384]{3,2,0,1:T(8,128)(2,1)S(1)} %fusion.38, bf16[1,4,160,384]{3,2,0,1:T(8,128)(2,1)S(1)} %get-tuple-element.10, bf16[1,4,160,384]{3,2,0,1:T(8,128)(2,1)S(1)} %get-tuple-element.9), kind=kLoop, calls=%fused_computation.18 | loop fusion | flops 20155392 | bytes 4451328 | tf_op jit(solution)/shard_map/broadcast_in_dim | solution.py:90
  119.0 1.7 %pad.5 = bf16[3,6,1,168,384]{4,3,0,1,2:T(8,128)(2,1)} pad(bf16[3,6,1,162,384]{4,3,0,1,2:T(8,128)(2,1)S(1)} %fusion.11, bf16[]{:T(256)} %constant.43.clone.1), padding=0_0x0_0x0_0x0_6x0_0 | pad | bytes 4561922 | tf_op jit(solution)/shard_map/broadcast_in_dim | solution.py:90
  120.6 3.5 %reshape.137 = bf16[3,6,1,8,21,384]{5,4,3,0,1,2:T(8,128)(2,1)S(1)} reshape(bf16[3,6,1,168,384]{4,3,0,1,2:T(8,128)(2,1)} %pad.5) | data formatting | bytes 4644864 | tf_op jit(solution)/shard_map/conv_general_dilated | solution.py:89
  124.2 0.0 copy-start.5
  124.2 0.0 copy-start.6
  124.2 0.3 copy.47
  124.5 0.1 slice.19
  124.6 1.7 %copy-done.5 = bf16[3,3,3,384,192]{3,4,2,1,0:T(8,128)(2,1)S(1)} copy-done((bf16[3,3,3,384,192]{3,4,2,1,0:T(8,128)(2,1)S(1)}, bf16[3,3,3,384,192]{3,4,2,1,0:T(8,128)(2,1)}, u32[]{:S(2)}) %copy-start.5) | copy-done | bytes 3981336
  126.3 0.0 copy-done.6
  126.3 3.9 %fusion.21 = f32[1,4,8,21,192]{4,2,3,1,0:T(8,128)S(1)} fusion(bf16[3,3,3,384,192]{3,4,2,1,0:T(8,128)(2,1)S(1)} %copy-done.5, bf16[3,6,1,7,2,384]{5,3,4,1,0,2:T(8,128)(2,1)S(1)} %slice.19, bf16[3,6,1,8,21,384]{5,3,4,1,0,2:T(8,128)(2,1)S(1)} %copy.47, pred[8,21]{0,1:T(8,128)(4,1)S(1)} %copy-done.6), kind=kOutput, calls=%fused_computation.29 | convolution fusion | flops 2683201536 | bytes 7013544 | tf_op jit(solution)/shard_map/conv_general_dilated | solution.py:89
  130.2 0.3 copy.48
  130.5 0.3 fusion.40
  130.8 0.8 copy.49
  (7 shorter events, 0.1 us)
Async XLA Ops:
  0.0 70.3 %copy-start = (bf16[384,384]{1,0:T(8,128)(2,1)S(1)}, bf16[384,384]{1,0:T(8,128)(2,1)}, u32[]{:S(2)}) copy-start(bf16[384,384]{1,0:T(8,128)(2,1)} %param.14) | copy-start | bytes 884740
  0.0 6.4 %copy-start.3 = (bf16[384]{0:T(512)(128)(2,1)S(1)}, bf16[384]{0:T(512)(128)(2,1)}, u32[]{:S(2)}) copy-start(bf16[384]{0:T(512)(128)(2,1)} %param.11) | copy-start | bytes 2308
  6.5 1.6 %collective-permute-start = (bf16[1,320,384]{2,1,0:T(8,128)(2,1)S(1)}, bf16[1,320,384]{2,1,0:T(8,128)(2,1)S(1)}, u32[]{:S(2)}, u32[]{:S(2)}) collective-permute-start(bf16[1,320,384]{2,1,0:T(8,128)(2,1)S(1)} %multiply_convert_fusion), channel_id=1, source_target_pairs={{0,1},{1,0},{4,5},{5,4},{8,9},{9,8},{12,13},{13,12},{2,3},{3,2},{6... | collective-permute-start | bytes 737288 | tf_op jit(solution)/shard_map/ppermute | solution.py:17
  8.3 14.6 %collective-permute-start.1 = (bf16[2,320,384]{2,1,0:T(8,128)(2,1)S(1)}, bf16[2,320,384]{2,1,0:T(8,128)(2,1)S(1)}, u32[]{:S(2)}, u32[]{:S(2)}) collective-permute-start(bf16[2,320,384]{2,1,0:T(8,128)(2,1)S(1)} %pad_maximum_fusion.2), channel_id=1, source_target_pairs={{0,4},{1,5},{4,0},{5,1},{8,12},{9,13},{12,8},{13,9},{2,6},{3,7},{6... | collective-permute-start | bytes 1474568 | tf_op jit(solution)/shard_map/ppermute | solution.py:17
  11.4 15.1 %copy-start.4 = (bf16[384]{0:T(512)(128)(2,1)S(1)}, bf16[384]{0:T(512)(128)(2,1)}, u32[]{:S(2)}) copy-start(bf16[384]{0:T(512)(128)(2,1)} %param.12) | copy-start | bytes 2308
  23.2 45.4 %collective-permute-start.2 = (bf16[4,320,384]{2,1,0:T(8,128)(2,1)S(1)}, bf16[4,320,384]{2,1,0:T(8,128)(2,1)}, u32[]{:S(2)}, u32[]{:S(2)}) collective-permute-start(bf16[4,320,384]{2,1,0:T(8,128)(2,1)S(1)} %pad_maximum_fusion.1), channel_id=1, source_target_pairs={{0,8},{1,9},{4,12},{5,13},{8,0},{9,1},{12,4},{13,5},{2,10},{3,11},... | collective-permute-start | bytes 2949128 | tf_op jit(solution)/shard_map/ppermute | solution.py:17
  76.8 4.2 %copy-start.2 = (bf16[384,384]{1,0:T(8,128)(2,1)S(1)}, bf16[384,384]{1,0:T(8,128)(2,1)}, u32[]{:S(2)}) copy-start(bf16[384,384]{1,0:T(8,128)(2,1)} %param.16) | copy-start | bytes 884740
  81.0 18.6 %copy-start.1 = (bf16[2,4,160,384]{3,2,1,0:T(8,128)(2,1)S(1)}, bf16[2,4,160,384]{3,2,1,0:T(8,128)(2,1)}, u32[]{:S(2)}) copy-start(bf16[2,4,160,384]{3,2,1,0:T(8,128)(2,1)} %param.10) | copy-start | bytes 2949124
  84.1 5.5 %collective-permute-start.3 = (bf16[1,4,160,384]{3,2,0,1:T(8,128)(2,1)S(1)}, bf16[1,4,160,384]{3,2,0,1:T(8,128)(2,1)}, u32[]{:S(2)}, u32[]{:S(2)}) collective-permute-start(bf16[1,4,160,384]{3,2,0,1:T(8,128)(2,1)S(1)} %fusion.38), channel_id=1, source_target_pairs={} | collective-permute-start | bytes 1474568 | tf_op jit(solution)/shard_map/ppermute | solution.py:29
  85.6 14.0 %collective-permute-start.4 = (bf16[1,4,160,384]{3,2,0,1:T(8,128)(2,1)S(1)}, bf16[1,4,160,384]{3,2,0,1:T(8,128)(2,1)}, u32[]{:S(2)}, u32[]{:S(2)}) collective-permute-start(bf16[1,4,160,384]{3,2,0,1:T(8,128)(2,1)S(1)} %fusion.38), channel_id=1, source_target_pairs={{0,2},{1,3},{4,6},{5,7},{8,10},{9,11},{12,14},{13,15},{16,18},{17,... | collective-permute-start | bytes 1474568 | tf_op jit(solution)/shard_map/ppermute | solution.py:29
  101.7 10.1 %collective-permute-start.5 = (bf16[3,1,160,384]{3,2,1,0:T(8,128)(2,1)}, bf16[3,1,160,384]{3,2,1,0:T(8,128)(2,1)S(1)}, u32[]{:S(2)}, u32[]{:S(2)}) collective-permute-start(bf16[3,1,160,384]{3,2,1,0:T(8,128)(2,1)} %get-tuple-element.7), channel_id=1, source_target_pairs={{0,4},{4,8},{8,12},{1,5},{5,9},{9,13},{2,6},{6,10},{10,14},{3,7},{... | collective-permute-start | bytes 1105928 | tf_op jit(solution)/shard_map/ppermute | solution.py:40
  104.2 11.7 %collective-permute-start.6 = (bf16[3,1,160,384]{3,2,1,0:T(8,128)(2,1)}, bf16[3,1,160,384]{3,2,1,0:T(8,128)(2,1)}, u32[]{:S(2)}, u32[]{:S(2)}) collective-permute-start(bf16[3,1,160,384]{3,2,1,0:T(8,128)(2,1)} %get-tuple-element.8), channel_id=1, source_target_pairs={{4,0},{8,4},{12,8},{5,1},{9,5},{13,9},{6,2},{10,6},{14,10},{7,3},{... | collective-permute-start | bytes 1105928 | tf_op jit(solution)/shard_map/ppermute | solution.py:42
  124.2 2.1 %copy-start.5 = (bf16[3,3,3,384,192]{3,4,2,1,0:T(8,128)(2,1)S(1)}, bf16[3,3,3,384,192]{3,4,2,1,0:T(8,128)(2,1)}, u32[]{:S(2)}) copy-start(bf16[3,3,3,384,192]{3,4,2,1,0:T(8,128)(2,1)} %param.17) | copy-start | bytes 11943940
  124.2 2.1 %copy-start.6 = (pred[8,21]{0,1:T(8,128)(4,1)S(1)}, pred[8,21]{0,1:T(8,128)(4,1)}, u32[]{:S(2)}) copy-start(pred[8,21]{0,1:T(8,128)(4,1)} %constant.51) | copy-start | bytes 508
